TPU v7x, 256 devices: a whole 4x4x8 slice. The times are simulated.
256 devices in a mesh: tile: 128 (over z_hi, x, y, core), member: 2 (over z_lo).
Axes of the slice: x: 4, y: 4, z: 8 (z_hi: 4, z_lo: 2; z = z_hi * 2 + z_lo), core: 2. Of those that a mesh axis runs over, the one named last changes fastest.
Arguments:
- fields: bfloat16 [2, 128, 2, 32, 32, 128], P('member', 'tile'), may hold values from -6 to 6
- cotangent: bfloat16 [2, 128, 2, 32, 32, 128], P('member', 'tile'), may hold values from -6 to 6
- edge_map: int32 [128, 4, 2], P('tile'), may hold values from 0 to 3, as said below
- w_first: bfloat16 [3, 3, 128, 128], replicated, may hold values from -0.1875 to 0.1875
- b_first: float32 [128], replicated, may hold values from -3 to 3
- w_second: bfloat16 [3, 3, 128, 128], replicated, may hold values from -0.1875 to 0.1875
- b_second: float32 [128], replicated, may hold values from -3 to 3
Outputs:
- response: bfloat16 [2, 128, 2, 32, 32, 128], P('member', 'tile')
- field_grad: bfloat16 [2, 128, 2, 32, 32, 128], P('member', 'tile')
- first_kernel_grad: float32 [3, 3, 128, 128], replicated
- first_bias_grad: float32 [128], replicated
- second_kernel_grad: float32 [3, 3, 128, 128], replicated
- second_bias_grad: float32 [128], replicated
Inputs may be any that keep to these rules, and one draw needn't show every extreme that they name: Each tile t is its own grid turned by r quarter turns: edge_map[t, g, 0] = (g - r) mod 4, and edge_map[t, g, 1] is 1 exactly when r = 2, or r = 1 and g is even, or r = 3 and g is odd.
All inputs are finite; a program needn't handle non-finite values.
Results may differ from a plain program's by a relative error of at most 0.0065.
Values may be sent and summed in bfloat16 or wider, within the bound.
A program may use at most 64 MiB of HBM per device.

v0:
```python
import jax
import jax.numpy as jnp
from jax import lax
from jax.sharding import PartitionSpec as P

ROW_TILES = 8
ROOT_HALF = 0.7071067811865476
INV_ROOT_TAU = 0.3989422804014327


def shifted(value, axis, steps):
    count = lax.axis_size(axis)
    pairs = [(source, (source + steps) % count) for source in range(count)]
    return lax.ppermute(value, axis, pairs)


def gelu_value(inputs):
    return 0.5 * inputs * (1.0 + jax.scipy.special.erf(inputs * ROOT_HALF))


def gelu_slope(inputs):
    return (
        0.5 * (1.0 + jax.scipy.special.erf(inputs * ROOT_HALF))
        + inputs * jnp.exp(-0.5 * inputs * inputs) * INV_ROOT_TAU
    )


def patches(padded):
    out_rows = padded.shape[-3] - 2
    out_cols = padded.shape[-2] - 2
    pieces = [
        padded[..., row_off : row_off + out_rows, col_off : col_off + out_cols, :]
        for row_off in range(3)
        for col_off in range(3)
    ]
    joined = jnp.concatenate(pieces, axis=-1)
    return joined.reshape(-1, joined.shape[-1])


def rim_strips(tile_data):
    return jnp.stack(
        [
            tile_data[..., 0, :, :],
            tile_data[..., :, -1, :],
            tile_data[..., -1, :, :],
            tile_data[..., :, 0, :],
        ],
        axis=-4,
    )


def orient(strips, chosen_ids, flip_ids):
    shaped_ids = chosen_ids.reshape(chosen_ids.shape + (1, 1, 1))
    shaped_flips = flip_ids.reshape(flip_ids.shape + (1, 1, 1))
    chosen = jnp.zeros_like(strips)
    for candidate in range(4):
        chosen = jnp.where(
            shaped_ids == candidate, jnp.expand_dims(strips[..., candidate, :, :, :], -4), chosen
        )
    flipped = chosen[..., ::-1, :]
    return jnp.where(shaped_flips == 1, flipped, chosen)


def assemble(tile_data, placed):
    top_rim = placed[..., 0, :, :, :]
    right_rim = placed[..., 1, :, :, :]
    bottom_rim = placed[..., 2, :, :, :]
    left_rim = placed[..., 3, :, :, :]
    kind = tile_data.dtype
    top_left = (
        0.5 * (top_rim[..., 0, :].astype(jnp.float32) + left_rim[..., 0, :].astype(jnp.float32))
    ).astype(kind)
    top_right = (
        0.5 * (top_rim[..., -1, :].astype(jnp.float32) + right_rim[..., 0, :].astype(jnp.float32))
    ).astype(kind)
    low_left = (
        0.5 * (bottom_rim[..., 0, :].astype(jnp.float32) + left_rim[..., -1, :].astype(jnp.float32))
    ).astype(kind)
    low_right = (
        0.5
        * (bottom_rim[..., -1, :].astype(jnp.float32) + right_rim[..., -1, :].astype(jnp.float32))
    ).astype(kind)
    top_row = jnp.concatenate([top_left[..., None, :], top_rim, top_right[..., None, :]], axis=-2)
    bottom_row = jnp.concatenate(
        [low_left[..., None, :], bottom_rim, low_right[..., None, :]], axis=-2
    )
    middle = jnp.concatenate(
        [left_rim[..., :, None, :], tile_data, right_rim[..., :, None, :]], axis=-2
    )
    return jnp.concatenate([top_row[..., None, :, :], middle, bottom_row[..., None, :, :]], axis=-3)


def fold_rims(grad_pad):
    interior = grad_pad[..., 1:-1, 1:-1, :]
    top_left = 0.5 * grad_pad[..., 0, 0, :]
    top_right = 0.5 * grad_pad[..., 0, -1, :]
    low_left = 0.5 * grad_pad[..., -1, 0, :]
    low_right = 0.5 * grad_pad[..., -1, -1, :]
    top_rim = grad_pad[..., 0, 1:-1, :].at[..., 0, :].add(top_left).at[..., -1, :].add(top_right)
    right_rim = (
        grad_pad[..., 1:-1, -1, :].at[..., 0, :].add(top_right).at[..., -1, :].add(low_right)
    )
    bottom_rim = (
        grad_pad[..., -1, 1:-1, :].at[..., 0, :].add(low_left).at[..., -1, :].add(low_right)
    )
    left_rim = grad_pad[..., 1:-1, 0, :].at[..., 0, :].add(top_left).at[..., -1, :].add(low_left)
    return (interior, jnp.stack([top_rim, right_rim, bottom_rim, left_rim], axis=-4))


def spread(interior, edge_grads):
    interior = interior.at[..., 0, :, :].add(edge_grads[..., 0, :, :, :])
    interior = interior.at[..., :, -1, :].add(edge_grads[..., 1, :, :, :])
    interior = interior.at[..., -1, :, :].add(edge_grads[..., 2, :, :, :])
    return interior.at[..., :, 0, :].add(edge_grads[..., 3, :, :, :])


def trade_rims(outgoing):
    offsets = (ROW_TILES, -1, -ROW_TILES, 1)
    received = []
    for direction in range(4):
        received.append(shifted(outgoing[(direction + 2) % 4], "tile", offsets[direction]))
    return jnp.stack(received)


def trade_grads(outgoing):
    offsets = (ROW_TILES, -1, -ROW_TILES, 1)
    received = []
    for direction in range(4):
        received.append(
            shifted(
                outgoing[(direction + 2) % 4].astype(jnp.bfloat16), "tile", offsets[direction]
            ).astype(jnp.float32)
        )
    return jnp.stack(received)


def pad_tile(tile_data, tables):
    side_ids, flip_marks, inverse, inverse_marks = tables
    outgoing = orient(rim_strips(tile_data), side_ids, flip_marks)
    incoming = trade_rims(outgoing)
    return assemble(tile_data, orient(incoming, inverse, inverse_marks))


def unpad_tile(grad_pad, tables):
    side_ids, flip_marks, inverse, inverse_marks = tables
    interior, placed = fold_rims(grad_pad)
    outgoing = orient(placed, side_ids, flip_marks)
    incoming = trade_grads(outgoing)
    return spread(interior, orient(incoming, inverse, inverse_marks))


def apply_cat(padded, weights_cat, out_rows, out_cols):
    product = jnp.dot(patches(padded), weights_cat, preferred_element_type=jnp.float32)
    return product.reshape(padded.shape[0], out_rows, out_cols, -1)


def forward_conv(tile_data, weights_cat, tables):
    tile_side = tile_data.shape[1]
    padded = pad_tile(tile_data, tables)
    result = apply_cat(padded, weights_cat, tile_side, tile_side)
    return (result, padded)


def back_conv(grad_data, weights_flip):
    tile_side = grad_data.shape[1]
    zero_pad = jnp.pad(grad_data, ((0, 0), (2, 2), (2, 2), (0, 0)))
    return apply_cat(zero_pad, weights_flip, tile_side + 2, tile_side + 2)


def kernel_term(padded, grad_data):
    channels = grad_data.shape[-1]
    total = lax.dot_general(
        patches(padded),
        grad_data.reshape(-1, channels),
        (((0,), (0,)), ((), ())),
        preferred_element_type=jnp.float32,
    )
    return total.reshape(3, 3, channels, channels)


def per_device(fields, cotangent, edge_map, w_first, b_first, w_second, b_second):
    frames, tile_side, channels = (fields.shape[2], fields.shape[3], fields.shape[5])
    source = fields.reshape(fields.shape[2:])
    upstream = cotangent.reshape(cotangent.shape[2:])
    side_ids = edge_map[0, :, 0]
    flip_marks = edge_map[0, :, 1]
    directions = jnp.arange(4, dtype=jnp.int32)
    inverse = jnp.sum(directions[None, :] * (side_ids[None, :] == directions[:, None]), axis=1)
    inverse_marks = jnp.take(flip_marks, inverse)
    tables = (side_ids, flip_marks, inverse, inverse_marks)
    first_cat = w_first.reshape(9 * channels, channels)
    second_cat = w_second.reshape(9 * channels, channels)
    first_flip = w_first[::-1, ::-1].transpose(0, 1, 3, 2).reshape(9 * channels, channels)
    second_flip = w_second[::-1, ::-1].transpose(0, 1, 3, 2).reshape(9 * channels, channels)
    norm_scale = float(
        lax.axis_size("tile") * lax.axis_size("member") * frames * tile_side * tile_side
    ) ** (-0.5)
    pre_one, pad_first = forward_conv(source, first_cat, tables)
    hidden_one = pre_one + b_first
    activity = gelu_value(hidden_one).astype(jnp.bfloat16)
    pre_two, pad_second = forward_conv(activity, second_cat, tables)
    hidden_two = pre_two + b_second
    response = gelu_value(hidden_two).astype(jnp.bfloat16)
    grad_second = (upstream.astype(jnp.float32) * gelu_slope(hidden_two)).astype(jnp.bfloat16)
    kernel_two = kernel_term(pad_second, grad_second)
    bias_two = jnp.sum(grad_second.astype(jnp.float32), axis=(0, 1, 2))
    grad_act = unpad_tile(back_conv(grad_second, second_flip), tables)
    grad_first = (grad_act * gelu_slope(hidden_one)).astype(jnp.bfloat16)
    kernel_one = kernel_term(pad_first, grad_first)
    bias_one = jnp.sum(grad_first.astype(jnp.float32), axis=(0, 1, 2))
    field_grad = unpad_tile(back_conv(grad_first, first_flip), tables).astype(jnp.bfloat16)
    kernel_one, bias_one, kernel_two, bias_two = lax.psum(
        (kernel_one, bias_one, kernel_two, bias_two), ("tile", "member")
    )
    return (
        response.reshape(fields.shape),
        field_grad.reshape(fields.shape),
        kernel_one * norm_scale,
        bias_one * norm_scale,
        kernel_two * norm_scale,
        bias_two * norm_scale,
    )


def solution(mesh):
    in_specs = (
        P("member", "tile", None, None, None, None),
        P("member", "tile", None, None, None, None),
        P("tile", None, None),
        P(),
        P(),
        P(),
        P(),
    )
    out_specs = (
        P("member", "tile", None, None, None, None),
        P("member", "tile", None, None, None, None),
        P(),
        P(),
        P(),
        P(),
    )
    return jax.shard_map(
        per_device, mesh=mesh, in_specs=in_specs, out_specs=out_specs, check_vma=False
    )
```

profile of v0, /device:TPU:2, one launch (start us, length us, event | category | flops | bytes accessed | tf_op | source)
XLA Modules:
  0.0 479.1 jit_solution(9307611065890658141)
XLA Ops:
  7.2 0.8 slice_bitcast_fusion.27
  8.0 1.0 fusion.81
  10.2 1.6 collective-permute-start.3
  11.8 3.5 collective-permute-start.2
  15.3 6.0 %collective-permute-start.1 = (bf16[2,32,128]{2,1,0:T(8,128)(2,1)S(1)}, bf16[2,32,128]{2,1,0:T(8,128)(2,1)S(1)}, u32[]{:S(2)}, u32[]{:S(2)}) collective-permute-start(bf16[2,32,128]{2,1,0:T(8,128)(2,1)S(1)} %get-tuple-element.401), channel_id=1, source_target_pairs={{0,240},{2,242},{4,244},{6,246},{8,248},{10,250},{12,252},{14,254}... | collective-permute-start | bytes 49160 | tf_op jit(solution)/shard_map/ppermute | solution.py:14
  22.9 1.2 copy.158
  24.8 1.2 copy.140
  27.7 1.1 fusion.79
  29.2 1.1 constant_dynamic-update-slice_fusion.5
  30.4 1.1 constant_dynamic-update-slice_fusion.3
  31.5 1.5 fusion.78
  33.5 1.4 fusion.84
  36.3 3.8 collective-permute-start.6
  40.0 6.2 %collective-permute-start.5 = (bf16[2,32,128]{2,1,0:T(8,128)(2,1)S(1)}, bf16[2,32,128]{2,1,0:T(8,128)(2,1)S(1)}, u32[]{:S(2)}, u32[]{:S(2)}) collective-permute-start(bf16[2,32,128]{2,1,0:T(8,128)(2,1)S(1)} %get-tuple-element.391), channel_id=1, source_target_pairs={{0,240},{2,242},{4,244},{6,246},{8,248},{10,250},{12,252},{14,254}... | collective-permute-start | bytes 49160 | tf_op jit(solution)/shard_map/ppermute | solution.py:14
  46.2 1.9 constant_dynamic-update-slice_fusion.18
  48.2 0.9 constant_dynamic-update-slice_fusion.17
  49.1 0.9 constant_dynamic-update-slice_fusion.16
  50.0 1.9 constant_dynamic-update-slice_fusion.15
  51.9 0.9 constant_dynamic-update-slice_fusion.14
  52.8 0.9 constant_dynamic-update-slice_fusion.13
  53.6 0.9 constant_dynamic-update-slice_fusion.12
  54.5 0.9 constant_dynamic-update-slice_fusion.11
  55.5 0.9 constant_dynamic-update-slice_fusion.10
  56.3 6.7 %copy.180 = bf16[1152,2048]{1,0:T(8,128)(2,1)} copy(bf16[1152,2048]{0,1:T(8,128)(2,1)} %bitcast.102) | data formatting | bytes 9437184 | tf_op jit(solution)/shard_map/dot_general | solution.py:172
  64.6 0.8 constant_dynamic-update-slice_fusion.9
  66.4 4.8 %copy.182 = bf16[2,32,32,1152]{3,2,1,0:T(8,128)(2,1)} copy(bf16[2,32,32,1152]{3,1,0,2:T(8,128)(2,1)S(1)} %slice_dynamic-update-slice_fusion) | data formatting | bytes 9437184 | tf_op jit(solution)/shard_map/concatenate | solution.py:36
  71.3 2.5 convert_reduce_fusion
  76.5 2.3 fusion.2
  80.7 6.7 %copy.183 = bf16[1152,2048]{1,0:T(8,128)(2,1)} copy(bf16[1152,2048]{0,1:T(8,128)(2,1)} %bitcast.263) | data formatting | bytes 9437184 | tf_op jit(solution)/shard_map/dot_general | solution.py:172
  88.2 0.8 copy.260
  93.7 1.4 select_select_fusion.3
  95.1 0.9 rev.35
  96.0 0.9 select_convert_fusion.1
  97.1 3.8 collective-permute-start.10
  100.8 6.0 %collective-permute-start.9 = (bf16[2,32,128]{2,1,0:T(8,128)(2,1)S(1)}, bf16[2,32,128]{2,1,0:T(8,128)(2,1)S(1)}, u32[]{:S(2)}, u32[]{:S(2)}) collective-permute-start(bf16[2,32,128]{2,1,0:T(8,128)(2,1)S(1)} %get-tuple-element.381), channel_id=1, source_target_pairs={{0,240},{2,242},{4,244},{6,246},{8,248},{10,250},{12,252},{14,254}... | collective-permute-start | bytes 49160 | tf_op jit(solution)/shard_map/ppermute | solution.py:14
  106.9 4.6 fusion.86
  111.6 1.1 copy.185
  113.8 0.9 convert_reduce_fusion.1
  117.4 2.1 fusion
  119.7 73.3 %all-reduce.2 = (f32[128]{0:T(128)S(1)}, f32[128]{0:T(128)S(1)}) all-reduce(f32[128]{0:T(128)S(1)} %get-tuple-element.318, f32[128]{0:T(128)S(1)} %copy-done.40), channel_id=1, replica_groups=mesh['tile'=128,'member'=2] {'tile','member'}, use_global_device_ids=true, to_apply=%region_3.4 | all-reduce | flops 256 | bytes 2048 | tf_op jit(solution)/shard_map/psum | solution.py:212
  194.1 2.3 collective-permute-start.15
  196.4 3.5 collective-permute-start.14
  199.9 5.4 %collective-permute-start.13 = (bf16[2,32,128]{2,1,0:T(8,128)(2,1)S(1)}, bf16[2,32,128]{2,1,0:T(8,128)(2,1)S(1)}, u32[]{:S(2)}, u32[]{:S(2)}) collective-permute-start(bf16[2,32,128]{2,1,0:T(8,128)(2,1)S(1)} %get-tuple-element.377), channel_id=1, source_target_pairs={{0,240},{2,242},{4,244},{6,246},{8,248},{10,250},{12,252},{14,254}... | collective-permute-start | bytes 49160 | tf_op jit(solution)/shard_map/ppermute | solution.py:14
  205.3 4.5 fusion.85
  211.7 1.1 copy.186
  212.8 255.2 %all-reduce.6.cloned.1.call-done = (f32[3,3,128,128]{3,2,1,0:T(8,128)}, f32[3,3,128,128]{3,2,1,0:T(8,128)}) async-done(((f32[3,3,128,128]{3,2,1,0:T(8,128)}, f32[3,3,128,128]{3,2,1,0:T(8,128)}), (f32[3,3,128,128]{3,2,1,0:T(8,128)}, f32[3,3,128,128]{3,2,1,0:T(8,128)})) %all-reduce.6.cloned.1.call-update) | async-done | bytes 1179664 | tf_op jit(solution)/shard_map/psum | solution.py:212
  468.0 1.9 broadcast_multiply_fusion.1
  469.9 1.9 broadcast_multiply_fusion
  (257 shorter events, 26.2 us)
Async XLA Ops:
  7.2 20.0 %copy-start = (bf16[1,1,2,32,32,128]{5,4,3,2,1,0:T(8,128)(2,1)S(1)}, bf16[1,1,2,32,32,128]{5,4,3,2,1,0:T(8,128)(2,1)}, u32[]{:S(2)}) copy-start(bf16[1,1,2,32,32,128]{5,4,3,2,1,0:T(8,128)(2,1)} %param.55) | copy-start | bytes 1572868
  7.2 460.8 %all-reduce.6.cloned.1.call-start = ((), (), s32[]{:S(2)}) async-start(), calls=%async_computation | async-start | bytes 2359296 | tf_op jit(solution)/shard_map/psum | solution.py:212
  9.8 26.1 %copy-start.22 = (pred[4]{0:T(512)(128)(4,1)}, pred[4]{0:T(512)(128)(4,1)S(1)}, u32[]{:S(2)}) copy-start(pred[4]{0:T(512)(128)(4,1)S(1)} %get-tuple-element.427) | copy-start | bytes 16
  9.8 26.1 %copy-start.24 = (pred[4]{0:T(512)(128)(4,1)}, pred[4]{0:T(512)(128)(4,1)S(1)}, u32[]{:S(2)}) copy-start(pred[4]{0:T(512)(128)(4,1)S(1)} %get-tuple-element.428) | copy-start | bytes 16
  9.8 26.1 %copy-start.26 = (pred[4]{0:T(512)(128)(4,1)}, pred[4]{0:T(512)(128)(4,1)S(1)}, u32[]{:S(2)}) copy-start(pred[4]{0:T(512)(128)(4,1)S(1)} %get-tuple-element.429) | copy-start | bytes 16
  9.8 26.1 %copy-start.28 = (pred[4]{0:T(512)(128)(4,1)}, pred[4]{0:T(512)(128)(4,1)S(1)}, u32[]{:S(2)}) copy-start(pred[4]{0:T(512)(128)(4,1)S(1)} %get-tuple-element.430) | copy-start | bytes 16
  9.8 26.1 %copy-start.32 = (pred[4]{0:T(512)(128)(4,1)}, pred[4]{0:T(512)(128)(4,1)S(1)}, u32[]{:S(2)}) copy-start(pred[4]{0:T(512)(128)(4,1)S(1)} %get-tuple-element.426) | copy-start | bytes 16
  10.1 16.6 %collective-permute-start = (bf16[2,32,128]{2,1,0:T(8,128)(2,1)S(1)}, bf16[2,32,128]{2,1,0:T(8,128)(2,1)S(1)}, u32[]{:S(2)}, u32[]{:S(2)}) collective-permute-start(bf16[2,32,128]{2,1,0:T(8,128)(2,1)S(1)} %get-tuple-element.398), channel_id=1, source_target_pairs={{0,2},{2,4},{4,6},{6,8},{8,10},{10,12},{12,14},{14,16},{16,18},{18... | collective-permute-start | bytes 49160 | tf_op jit(solution)/shard_map/ppermute | solution.py:14
  10.2 16.5 %collective-permute-start.3 = (bf16[2,32,128]{2,1,0:T(8,128)(2,1)S(1)}, bf16[2,32,128]{2,1,0:T(8,128)(2,1)S(1)}, u32[]{:S(2)}, u32[]{:S(2)}) collective-permute-start(bf16[2,32,128]{2,1,0:T(8,128)(2,1)S(1)} %get-tuple-element.399), channel_id=1, source_target_pairs={{0,16},{2,18},{4,20},{6,22},{8,24},{10,26},{12,28},{14,30},{16,32}... | collective-permute-start | bytes 49160 | tf_op jit(solution)/shard_map/ppermute | solution.py:14
  11.8 15.0 %collective-permute-start.2 = (bf16[2,32,128]{2,1,0:T(8,128)(2,1)S(1)}, bf16[2,32,128]{2,1,0:T(8,128)(2,1)S(1)}, u32[]{:S(2)}, u32[]{:S(2)}) collective-permute-start(bf16[2,32,128]{2,1,0:T(8,128)(2,1)S(1)} %get-tuple-element.400), channel_id=1, source_target_pairs={{0,254},{2,0},{4,2},{6,4},{8,6},{10,8},{12,10},{14,12},{16,14},{18... | collective-permute-start | bytes 49160 | tf_op jit(solution)/shard_map/ppermute | solution.py:14
  15.3 11.5 %collective-permute-start.1 = (bf16[2,32,128]{2,1,0:T(8,128)(2,1)S(1)}, bf16[2,32,128]{2,1,0:T(8,128)(2,1)S(1)}, u32[]{:S(2)}, u32[]{:S(2)}) collective-permute-start(bf16[2,32,128]{2,1,0:T(8,128)(2,1)S(1)} %get-tuple-element.401), channel_id=1, source_target_pairs={{0,240},{2,242},{4,244},{6,246},{8,248},{10,250},{12,252},{14,254}... | collective-permute-start | bytes 49160 | tf_op jit(solution)/shard_map/ppermute | solution.py:14
  22.8 40.4 %copy-start.14 = (pred[4]{0:T(512)(128)(4,1)}, pred[4]{0:T(512)(128)(4,1)S(1)}, u32[]{:S(2)}) copy-start(pred[4]{0:T(512)(128)(4,1)S(1)} %get-tuple-element.432) | copy-start | bytes 16
  22.8 40.4 %copy-start.16 = (pred[4]{0:T(512)(128)(4,1)}, pred[4]{0:T(512)(128)(4,1)S(1)}, u32[]{:S(2)}) copy-start(pred[4]{0:T(512)(128)(4,1)S(1)} %get-tuple-element.433) | copy-start | bytes 16
  22.9 40.4 %copy-start.18 = (pred[4]{0:T(512)(128)(4,1)}, pred[4]{0:T(512)(128)(4,1)S(1)}, u32[]{:S(2)}) copy-start(pred[4]{0:T(512)(128)(4,1)S(1)} %get-tuple-element.434) | copy-start | bytes 16
  22.9 40.4 %copy-start.20 = (pred[4]{0:T(512)(128)(4,1)}, pred[4]{0:T(512)(128)(4,1)S(1)}, u32[]{:S(2)}) copy-start(pred[4]{0:T(512)(128)(4,1)S(1)} %get-tuple-element.435) | copy-start | bytes 16
  22.9 40.4 %copy-start.30 = (pred[4]{0:T(512)(128)(4,1)}, pred[4]{0:T(512)(128)(4,1)S(1)}, u32[]{:S(2)}) copy-start(pred[4]{0:T(512)(128)(4,1)S(1)} %get-tuple-element.431) | copy-start | bytes 16
  29.2 4.3 copy-start.5
  36.0 16.8 %copy-start.2 = (bf16[2,32,32,128]{3,2,1,0:T(8,128)(2,1)S(1)}, bf16[2,32,32,128]{3,2,1,0:T(8,128)(2,1)}, u32[]{:S(2)}) copy-start(bf16[2,32,32,128]{3,2,1,0:T(8,128)(2,1)} %get-tuple-element.321) | copy-start | bytes 1572868
  36.0 17.7 %copy-start.4 = (bf16[2,32,32,128]{3,2,1,0:T(8,128)(2,1)S(1)}, bf16[2,32,32,128]{3,2,1,0:T(8,128)(2,1)}, u32[]{:S(2)}) copy-start(bf16[2,32,32,128]{3,2,1,0:T(8,128)(2,1)} %get-tuple-element.353) | copy-start | bytes 1572868
  36.0 18.5 %copy-start.3 = (bf16[2,32,32,128]{3,2,1,0:T(8,128)(2,1)S(1)}, bf16[2,32,32,128]{3,2,1,0:T(8,128)(2,1)}, u32[]{:S(2)}) copy-start(bf16[2,32,32,128]{3,2,1,0:T(8,128)(2,1)} %get-tuple-element.352) | copy-start | bytes 1572868
  36.0 19.5 %copy-start.1 = (bf16[2,32,32,128]{3,2,1,0:T(8,128)(2,1)S(1)}, bf16[2,32,32,128]{3,2,1,0:T(8,128)(2,1)}, u32[]{:S(2)}) copy-start(bf16[2,32,32,128]{3,2,1,0:T(8,128)(2,1)} %get-tuple-element.350) | copy-start | bytes 1572868
  36.1 27.0 %collective-permute-start.4 = (bf16[2,32,128]{2,1,0:T(8,128)(2,1)S(1)}, bf16[2,32,128]{2,1,0:T(8,128)(2,1)S(1)}, u32[]{:S(2)}, u32[]{:S(2)}) collective-permute-start(bf16[2,32,128]{2,1,0:T(8,128)(2,1)S(1)} %get-tuple-element.388), channel_id=1, source_target_pairs={{0,2},{2,4},{4,6},{6,8},{8,10},{10,12},{12,14},{14,16},{16,18},{18... | collective-permute-start | bytes 49160 | tf_op jit(solution)/shard_map/ppermute | solution.py:14
  36.2 26.9 %collective-permute-start.7 = (bf16[2,32,128]{2,1,0:T(8,128)(2,1)S(1)}, bf16[2,32,128]{2,1,0:T(8,128)(2,1)S(1)}, u32[]{:S(2)}, u32[]{:S(2)}) collective-permute-start(bf16[2,32,128]{2,1,0:T(8,128)(2,1)S(1)} %get-tuple-element.389), channel_id=1, source_target_pairs={{0,16},{2,18},{4,20},{6,22},{8,24},{10,26},{12,28},{14,30},{16,32}... | collective-permute-start | bytes 49160 | tf_op jit(solution)/shard_map/ppermute | solution.py:14
  36.3 26.8 %collective-permute-start.6 = (bf16[2,32,128]{2,1,0:T(8,128)(2,1)S(1)}, bf16[2,32,128]{2,1,0:T(8,128)(2,1)S(1)}, u32[]{:S(2)}, u32[]{:S(2)}) collective-permute-start(bf16[2,32,128]{2,1,0:T(8,128)(2,1)S(1)} %get-tuple-element.390), channel_id=1, source_target_pairs={{0,254},{2,0},{4,2},{6,4},{8,6},{10,8},{12,10},{14,12},{16,14},{18... | collective-permute-start | bytes 49160 | tf_op jit(solution)/shard_map/ppermute | solution.py:14
  40.0 23.0 %collective-permute-start.5 = (bf16[2,32,128]{2,1,0:T(8,128)(2,1)S(1)}, bf16[2,32,128]{2,1,0:T(8,128)(2,1)S(1)}, u32[]{:S(2)}, u32[]{:S(2)}) collective-permute-start(bf16[2,32,128]{2,1,0:T(8,128)(2,1)S(1)} %get-tuple-element.391), channel_id=1, source_target_pairs={{0,240},{2,242},{4,244},{6,246},{8,248},{10,250},{12,252},{14,254}... | collective-permute-start | bytes 49160 | tf_op jit(solution)/shard_map/ppermute | solution.py:14
  66.4 4.9 %copy-start.6 = (bf16[3,3,128,128]{3,2,1,0:T(8,128)(2,1)S(1)}, bf16[3,3,128,128]{3,2,1,0:T(8,128)(2,1)}, u32[]{:S(2)}) copy-start(bf16[3,3,128,128]{3,2,1,0:T(8,128)(2,1)} %param.60) | copy-start | bytes 884740
  66.4 4.9 %copy-start.38 = (bf16[1,1,2,32,32,128]{5,4,3,2,1,0:T(8,128)(2,1)S(1)}, bf16[1,1,2,32,32,128]{5,4,3,2,1,0:T(8,128)(2,1)}, u32[]{:S(2)}) copy-start(bf16[1,1,2,32,32,128]{5,4,3,2,1,0:T(8,128)(2,1)} %param.56) | copy-start | bytes 1572868
  66.4 4.9 %copy-start.39 = (f32[128]{0:T(128)S(1)}, f32[128]{0:T(128)}, u32[]{:S(2)}) copy-start(f32[128]{0:T(128)} %param.61) | copy-start | bytes 1540
  96.9 15.9 %collective-permute-start.8 = (bf16[2,32,128]{2,1,0:T(8,128)(2,1)S(1)}, bf16[2,32,128]{2,1,0:T(8,128)(2,1)S(1)}, u32[]{:S(2)}, u32[]{:S(2)}) collective-permute-start(bf16[2,32,128]{2,1,0:T(8,128)(2,1)S(1)} %get-tuple-element.378), channel_id=1, source_target_pairs={{0,2},{2,4},{4,6},{6,8},{8,10},{10,12},{12,14},{14,16},{16,18},{18... | collective-permute-start | bytes 49160 | tf_op jit(solution)/shard_map/ppermute | solution.py:14
  97.0 15.8 %collective-permute-start.11 = (bf16[2,32,128]{2,1,0:T(8,128)(2,1)S(1)}, bf16[2,32,128]{2,1,0:T(8,128)(2,1)S(1)}, u32[]{:S(2)}, u32[]{:S(2)}) collective-permute-start(bf16[2,32,128]{2,1,0:T(8,128)(2,1)S(1)} %get-tuple-element.379), channel_id=1, source_target_pairs={{0,16},{2,18},{4,20},{6,22},{8,24},{10,26},{12,28},{14,30},{16,32}... | collective-permute-start | bytes 49160 | tf_op jit(solution)/shard_map/ppermute | solution.py:14
  97.1 15.8 %collective-permute-start.10 = (bf16[2,32,128]{2,1,0:T(8,128)(2,1)S(1)}, bf16[2,32,128]{2,1,0:T(8,128)(2,1)S(1)}, u32[]{:S(2)}, u32[]{:S(2)}) collective-permute-start(bf16[2,32,128]{2,1,0:T(8,128)(2,1)S(1)} %get-tuple-element.380), channel_id=1, source_target_pairs={{0,254},{2,0},{4,2},{6,4},{8,6},{10,8},{12,10},{14,12},{16,14},{18... | collective-permute-start | bytes 49160 | tf_op jit(solution)/shard_map/ppermute | solution.py:14
  100.8 12.0 %collective-permute-start.9 = (bf16[2,32,128]{2,1,0:T(8,128)(2,1)S(1)}, bf16[2,32,128]{2,1,0:T(8,128)(2,1)S(1)}, u32[]{:S(2)}, u32[]{:S(2)}) collective-permute-start(bf16[2,32,128]{2,1,0:T(8,128)(2,1)S(1)} %get-tuple-element.381), channel_id=1, source_target_pairs={{0,240},{2,242},{4,244},{6,246},{8,248},{10,250},{12,252},{14,254}... | collective-permute-start | bytes 49160 | tf_op jit(solution)/shard_map/ppermute | solution.py:14
  106.8 6.1 %copy-start.15 = (pred[4]{0:T(512)(128)(4,1)S(1)}, pred[4]{0:T(512)(128)(4,1)}, u32[]{:S(2)}) copy-start(pred[4]{0:T(512)(128)(4,1)} %copy-done.14) | copy-start | bytes 16
  106.8 6.1 %copy-start.17 = (pred[4]{0:T(512)(128)(4,1)S(1)}, pred[4]{0:T(512)(128)(4,1)}, u32[]{:S(2)}) copy-start(pred[4]{0:T(512)(128)(4,1)} %copy-done.16) | copy-start | bytes 16
  106.8 6.1 %copy-start.19 = (pred[4]{0:T(512)(128)(4,1)S(1)}, pred[4]{0:T(512)(128)(4,1)}, u32[]{:S(2)}) copy-start(pred[4]{0:T(512)(128)(4,1)} %copy-done.18) | copy-start | bytes 16
  106.8 6.1 %copy-start.21 = (pred[4]{0:T(512)(128)(4,1)S(1)}, pred[4]{0:T(512)(128)(4,1)}, u32[]{:S(2)}) copy-start(pred[4]{0:T(512)(128)(4,1)} %copy-done.20) | copy-start | bytes 16
  106.8 6.2 %copy-start.31 = (pred[4]{0:T(512)(128)(4,1)S(1)}, pred[4]{0:T(512)(128)(4,1)}, u32[]{:S(2)}) copy-start(pred[4]{0:T(512)(128)(4,1)} %copy-done.30) | copy-start | bytes 16
  111.4 2.3 copy-start.37
  117.4 76.2 %copy-start.35 = (f32[2,1,1,128]{3,1,2,0:T(1,128)S(1)}, f32[2,1,1,128]{3,1,2,0:T(1,128)}, u32[]{:S(2)}) copy-start(f32[2,1,1,128]{3,1,2,0:T(1,128)} %copy-done.34) | copy-start | bytes 3076
  117.4 76.3 %copy-start.23 = (pred[4]{0:T(512)(128)(4,1)S(1)}, pred[4]{0:T(512)(128)(4,1)}, u32[]{:S(2)}) copy-start(pred[4]{0:T(512)(128)(4,1)} %copy-done.22) | copy-start | bytes 16
  117.4 76.3 %copy-start.25 = (pred[4]{0:T(512)(128)(4,1)S(1)}, pred[4]{0:T(512)(128)(4,1)}, u32[]{:S(2)}) copy-start(pred[4]{0:T(512)(128)(4,1)} %copy-done.24) | copy-start | bytes 16
  117.4 76.3 %copy-start.27 = (pred[4]{0:T(512)(128)(4,1)S(1)}, pred[4]{0:T(512)(128)(4,1)}, u32[]{:S(2)}) copy-start(pred[4]{0:T(512)(128)(4,1)} %copy-done.26) | copy-start | bytes 16
  117.4 76.3 %copy-start.29 = (pred[4]{0:T(512)(128)(4,1)S(1)}, pred[4]{0:T(512)(128)(4,1)}, u32[]{:S(2)}) copy-start(pred[4]{0:T(512)(128)(4,1)} %copy-done.28) | copy-start | bytes 16
  117.4 76.5 %copy-start.33 = (pred[4]{0:T(512)(128)(4,1)S(1)}, pred[4]{0:T(512)(128)(4,1)}, u32[]{:S(2)}) copy-start(pred[4]{0:T(512)(128)(4,1)} %copy-done.32) | copy-start | bytes 16
  194.0 16.6 %collective-permute-start.12 = (bf16[2,32,128]{2,1,0:T(8,128)(2,1)S(1)}, bf16[2,32,128]{2,1,0:T(8,128)(2,1)S(1)}, u32[]{:S(2)}, u32[]{:S(2)}) collective-permute-start(bf16[2,32,128]{2,1,0:T(8,128)(2,1)S(1)} %get-tuple-element.374), channel_id=1, source_target_pairs={{0,2},{2,4},{4,6},{6,8},{8,10},{10,12},{12,14},{14,16},{16,18},{18... | collective-permute-start | bytes 49160 | tf_op jit(solution)/shard_map/ppermute | solution.py:14
  194.1 16.6 %collective-permute-start.15 = (bf16[2,32,128]{2,1,0:T(8,128)(2,1)S(1)}, bf16[2,32,128]{2,1,0:T(8,128)(2,1)S(1)}, u32[]{:S(2)}, u32[]{:S(2)}) collective-permute-start(bf16[2,32,128]{2,1,0:T(8,128)(2,1)S(1)} %get-tuple-element.375), channel_id=1, source_target_pairs={{0,16},{2,18},{4,20},{6,22},{8,24},{10,26},{12,28},{14,30},{16,32}... | collective-permute-start | bytes 49160 | tf_op jit(solution)/shard_map/ppermute | solution.py:14
  196.4 14.3 %collective-permute-start.14 = (bf16[2,32,128]{2,1,0:T(8,128)(2,1)S(1)}, bf16[2,32,128]{2,1,0:T(8,128)(2,1)S(1)}, u32[]{:S(2)}, u32[]{:S(2)}) collective-permute-start(bf16[2,32,128]{2,1,0:T(8,128)(2,1)S(1)} %get-tuple-element.376), channel_id=1, source_target_pairs={{0,254},{2,0},{4,2},{6,4},{8,6},{10,8},{12,10},{14,12},{16,14},{18... | collective-permute-start | bytes 49160 | tf_op jit(solution)/shard_map/ppermute | solution.py:14
  199.9 10.8 %collective-permute-start.13 = (bf16[2,32,128]{2,1,0:T(8,128)(2,1)S(1)}, bf16[2,32,128]{2,1,0:T(8,128)(2,1)S(1)}, u32[]{:S(2)}, u32[]{:S(2)}) collective-permute-start(bf16[2,32,128]{2,1,0:T(8,128)(2,1)S(1)} %get-tuple-element.377), channel_id=1, source_target_pairs={{0,240},{2,242},{4,244},{6,246},{8,248},{10,250},{12,252},{14,254}... | collective-permute-start | bytes 49160 | tf_op jit(solution)/shard_map/ppermute | solution.py:14
  (10 other events, 15.0 us)
Sparse Core Ops, SparseCore 0:
  210.8 257.1 all-reduce.5
where the time goes:
time: 489 us; the launch traced here: 479 us
  waiting for transfers between devices  255 us (52%)
  blocking collectives  73.3 us (15%)
  local copies, waits for them, and re-layouts  56.4 us (12%)
  starting transfers between devices  42.5 us (9%)
  other arithmetic  18.3 us (4%)
  matrix products  17.4 us (4%)
  between operations  15.9 us (3%)
    psum x1, waiting for transfers between devices, per_device(): lax.psum((kernel_one, bias_one, kernel_two, bias_two), ('tile', 'member'))  255 us
    psum x1, blocking collectives, per_device(): lax.psum((kernel_one, bias_one, kernel_two, bias_two), ('tile', 'member'))  73.3 us
    ppermute x16, starting transfers between devices, shifted(): return lax.ppermute(value, axis, pairs)  42.5 us
    unnamed x134, local copies, waits for them, and re-layouts  23.3 us
    dot_general x2, local copies, waits for them, and re-layouts, kernel_term(): lax.dot_general(patches(padded), grad_data.reshape(-1, channels), (((0,),...  13.4 us
  transfers between devices with their start and end apart: 17, of which 1 were waited for; matrix products, arithmetic and copies ran while one was open for 7% of the time, Pallas kernels for 0%

commit v1 on v0

--- a/solution.py
+++ b/solution.py
@@ -2,6 +2,7 @@
 import jax.numpy as jnp
 from jax import lax
 from jax.sharding import PartitionSpec as P
+from jax.lax import psum
 
 ROW_TILES = 8
 ROOT_HALF = 0.7071067811865476
@@ -209,8 +210,9 @@
     kernel_one = kernel_term(pad_first, grad_first)
     bias_one = jnp.sum(grad_first.astype(jnp.float32), axis=(0, 1, 2))
     field_grad = unpad_tile(back_conv(grad_first, first_flip), tables).astype(jnp.bfloat16)
-    kernel_one, bias_one, kernel_two, bias_two = lax.psum(
-        (kernel_one, bias_one, kernel_two, bias_two), ("tile", "member")
+    compute_gates = lambda message: psum(psum(message, axis_name="tile"), axis_name="member")
+    kernel_one, bias_one, kernel_two, bias_two = compute_gates(
+        (kernel_one, bias_one, kernel_two, bias_two)
     )
     return (
         response.reshape(fields.shape),

time: 489 us -> 1480 us (3.03)
  waiting for transfers between devices: 255 us -> 998 us
  blocking collectives: 73.3 us -> 320 us
    psum x1 -> x2, waiting for transfers between devices: 255 us -> 998 us  [the longest x1 926 us: per_device(): psum(message, axis_name='tile')]
    psum x1 -> x2, blocking collectives: 73.3 us -> 320 us  [the longest x1 315 us: per_device(): psum(message, axis_name='tile')]
  transfers between devices with their start and end apart: 17 -> 18, of which waited for: 1 -> 2; matrix products, arithmetic and copies ran while one was open for 7% -> 2% of each run, Pallas kernels for 0% -> 0%
where the time goes in v1:
time: 1480 us; the launch traced here: 1470 us
  waiting for transfers between devices  998 us (67%)
  blocking collectives  320 us (22%)
  local copies, waits for them, and re-layouts  56.4 us (4%)
  starting transfers between devices  41.2 us (3%)
  other arithmetic  18.3 us (1%)
  matrix products  17.4 us (1%)
  between operations  16 us (1%)
    psum x1, waiting for transfers between devices, per_device(): psum(message, axis_name='tile')  926 us
    psum x1, blocking collectives, per_device(): psum(message, axis_name='tile')  315 us
    psum x1, waiting for transfers between devices, per_device(): psum(psum(message, axis_name='tile'), axis_name='member')  72 us
    ppermute x16, starting transfers between devices, shifted(): return lax.ppermute(value, axis, pairs)  41.1 us
  transfers between devices with their start and end apart: 18, of which 2 were waited for; matrix products, arithmetic and copies ran while one was open for 2% of the time, Pallas kernels for 0%

profile of v1, /device:TPU:2, one launch (start us, length us, event | category | flops | bytes accessed | tf_op | source)
XLA Modules:
  0.0 1466.6 jit_solution(12651013485872004654)
XLA Ops:
  7.2 0.8 slice_bitcast_fusion.27
  8.0 1.0 fusion.81
  10.2 1.6 collective-permute-start.3
  11.8 3.5 collective-permute-start.2
  15.3 6.0 collective-permute-start.1
  22.9 1.2 copy.158
  24.8 1.2 copy.140
  27.6 1.1 fusion.79
  29.2 1.1 constant_dynamic-update-slice_fusion.5
  30.4 1.1 constant_dynamic-update-slice_fusion.3
  31.5 1.5 fusion.78
  33.5 1.4 fusion.84
  36.3 3.8 collective-permute-start.6
  40.0 6.2 collective-permute-start.5
  46.2 1.9 constant_dynamic-update-slice_fusion.18
  48.1 0.9 constant_dynamic-update-slice_fusion.17
  49.1 0.9 constant_dynamic-update-slice_fusion.16
  50.0 1.9 constant_dynamic-update-slice_fusion.15
  51.9 0.9 constant_dynamic-update-slice_fusion.14
  52.8 0.9 constant_dynamic-update-slice_fusion.13
  53.6 0.9 constant_dynamic-update-slice_fusion.12
  54.5 0.9 constant_dynamic-update-slice_fusion.11
  55.5 0.9 constant_dynamic-update-slice_fusion.10
  56.3 6.7 copy.180
  64.6 0.8 constant_dynamic-update-slice_fusion.9
  66.4 4.8 copy.182
  71.2 2.5 convert_reduce_fusion
  76.5 2.3 fusion.2
  80.7 6.7 copy.183
  93.7 1.4 select_select_fusion.3
  95.1 0.9 rev.35
  96.0 0.9 select_convert_fusion.1
  97.1 3.8 collective-permute-start.10
  100.8 6.0 collective-permute-start.9
  106.8 4.5 fusion.86
  111.5 1.1 copy.185
  113.7 0.9 convert_reduce_fusion.1
  117.4 2.1 fusion
  120.1 4.5 fusion.85
  125.0 3.8 collective-permute-start.14
  128.8 6.0 collective-permute-start.13
  134.8 314.7 %all-reduce.2 = (f32[128]{0:T(128)S(1)}, f32[128]{0:T(128)S(1)}) all-reduce(f32[128]{0:T(128)S(1)} %get-tuple-element.322, f32[128]{0:T(128)S(1)} %copy-done.40), channel_id=1, replica_groups=mesh['tile'=128,'member'=2] {'tile'}, use_global_device_ids=true, to_apply=%region_4.5 | all-reduce | flops 256 | bytes 2048 | tf_op jit(solution)/shard_map/psum | solution.py:213
  449.5 4.9 all-reduce.4
  456.0 925.7 %all-reduce.9.cloned.1.call-done = (f32[3,3,128,128]{3,2,1,0:T(8,128)}, f32[3,3,128,128]{3,2,1,0:T(8,128)}) async-done(((f32[3,3,128,128]{3,2,1,0:T(8,128)}, f32[3,3,128,128]{3,2,1,0:T(8,128)}), (f32[3,3,128,128]{3,2,1,0:T(8,128)}, f32[3,3,128,128]{3,2,1,0:T(8,128)})) %all-reduce.9.cloned.1.call-update) | async-done | bytes 1179664 | tf_op jit(solution)/shard_map/psum | solution.py:213
  1382.4 1.1 copy.186
  1383.5 72.0 %all-reduce.11.cloned.1.call-done = (f32[3,3,128,128]{3,2,1,0:T(8,128)}, f32[3,3,128,128]{3,2,1,0:T(8,128)}) async-done(((f32[3,3,128,128]{3,2,1,0:T(8,128)}, f32[3,3,128,128]{3,2,1,0:T(8,128)}), (f32[3,3,128,128]{3,2,1,0:T(8,128)}, f32[3,3,128,128]{3,2,1,0:T(8,128)})) %all-reduce.11.cloned.1.call-update) | async-done | bytes 1179664 | tf_op jit(solution)/shard_map/psum | solution.py:213
  1455.5 1.9 broadcast_multiply_fusion.1
  1457.5 1.9 broadcast_multiply_fusion
  (261 shorter events, 27.2 us)
Async XLA Ops:
  7.2 20.0 %copy-start = (bf16[1,1,2,32,32,128]{5,4,3,2,1,0:T(8,128)(2,1)S(1)}, bf16[1,1,2,32,32,128]{5,4,3,2,1,0:T(8,128)(2,1)}, u32[]{:S(2)}) copy-start(bf16[1,1,2,32,32,128]{5,4,3,2,1,0:T(8,128)(2,1)} %param.55) | copy-start | bytes 1572868
  7.2 1374.5 %all-reduce.9.cloned.1.call-start = ((), (), s32[]{:S(2)}) async-start(), calls=%async_computation | async-start | bytes 2359296 | tf_op jit(solution)/shard_map/psum | solution.py:213
  9.8 26.1 %copy-start.22 = (pred[4]{0:T(512)(128)(4,1)}, pred[4]{0:T(512)(128)(4,1)S(1)}, u32[]{:S(2)}) copy-start(pred[4]{0:T(512)(128)(4,1)S(1)} %get-tuple-element.431) | copy-start | bytes 16
  9.8 26.1 %copy-start.24 = (pred[4]{0:T(512)(128)(4,1)}, pred[4]{0:T(512)(128)(4,1)S(1)}, u32[]{:S(2)}) copy-start(pred[4]{0:T(512)(128)(4,1)S(1)} %get-tuple-element.432) | copy-start | bytes 16
  9.8 26.1 %copy-start.26 = (pred[4]{0:T(512)(128)(4,1)}, pred[4]{0:T(512)(128)(4,1)S(1)}, u32[]{:S(2)}) copy-start(pred[4]{0:T(512)(128)(4,1)S(1)} %get-tuple-element.433) | copy-start | bytes 16
  9.8 26.1 %copy-start.28 = (pred[4]{0:T(512)(128)(4,1)}, pred[4]{0:T(512)(128)(4,1)S(1)}, u32[]{:S(2)}) copy-start(pred[4]{0:T(512)(128)(4,1)S(1)} %get-tuple-element.434) | copy-start | bytes 16
  9.8 26.1 %copy-start.32 = (pred[4]{0:T(512)(128)(4,1)}, pred[4]{0:T(512)(128)(4,1)S(1)}, u32[]{:S(2)}) copy-start(pred[4]{0:T(512)(128)(4,1)S(1)} %get-tuple-element.430) | copy-start | bytes 16
  10.1 16.6 %collective-permute-start = (bf16[2,32,128]{2,1,0:T(8,128)(2,1)S(1)}, bf16[2,32,128]{2,1,0:T(8,128)(2,1)S(1)}, u32[]{:S(2)}, u32[]{:S(2)}) collective-permute-start(bf16[2,32,128]{2,1,0:T(8,128)(2,1)S(1)} %get-tuple-element.402), channel_id=1, source_target_pairs={{0,2},{2,4},{4,6},{6,8},{8,10},{10,12},{12,14},{14,16},{16,18},{18... | collective-permute-start | bytes 49160 | tf_op jit(solution)/shard_map/ppermute | solution.py:15
  10.2 16.5 %collective-permute-start.3 = (bf16[2,32,128]{2,1,0:T(8,128)(2,1)S(1)}, bf16[2,32,128]{2,1,0:T(8,128)(2,1)S(1)}, u32[]{:S(2)}, u32[]{:S(2)}) collective-permute-start(bf16[2,32,128]{2,1,0:T(8,128)(2,1)S(1)} %get-tuple-element.403), channel_id=1, source_target_pairs={{0,16},{2,18},{4,20},{6,22},{8,24},{10,26},{12,28},{14,30},{16,32}... | collective-permute-start | bytes 49160 | tf_op jit(solution)/shard_map/ppermute | solution.py:15
  11.8 15.0 %collective-permute-start.2 = (bf16[2,32,128]{2,1,0:T(8,128)(2,1)S(1)}, bf16[2,32,128]{2,1,0:T(8,128)(2,1)S(1)}, u32[]{:S(2)}, u32[]{:S(2)}) collective-permute-start(bf16[2,32,128]{2,1,0:T(8,128)(2,1)S(1)} %get-tuple-element.404), channel_id=1, source_target_pairs={{0,254},{2,0},{4,2},{6,4},{8,6},{10,8},{12,10},{14,12},{16,14},{18... | collective-permute-start | bytes 49160 | tf_op jit(solution)/shard_map/ppermute | solution.py:15
  15.3 11.5 collective-permute-start.1
  22.8 40.4 %copy-start.14 = (pred[4]{0:T(512)(128)(4,1)}, pred[4]{0:T(512)(128)(4,1)S(1)}, u32[]{:S(2)}) copy-start(pred[4]{0:T(512)(128)(4,1)S(1)} %get-tuple-element.436) | copy-start | bytes 16
  22.8 40.4 %copy-start.16 = (pred[4]{0:T(512)(128)(4,1)}, pred[4]{0:T(512)(128)(4,1)S(1)}, u32[]{:S(2)}) copy-start(pred[4]{0:T(512)(128)(4,1)S(1)} %get-tuple-element.437) | copy-start | bytes 16
  22.9 40.4 %copy-start.18 = (pred[4]{0:T(512)(128)(4,1)}, pred[4]{0:T(512)(128)(4,1)S(1)}, u32[]{:S(2)}) copy-start(pred[4]{0:T(512)(128)(4,1)S(1)} %get-tuple-element.438) | copy-start | bytes 16
  22.9 40.4 %copy-start.20 = (pred[4]{0:T(512)(128)(4,1)}, pred[4]{0:T(512)(128)(4,1)S(1)}, u32[]{:S(2)}) copy-start(pred[4]{0:T(512)(128)(4,1)S(1)} %get-tuple-element.439) | copy-start | bytes 16
  22.9 40.4 %copy-start.30 = (pred[4]{0:T(512)(128)(4,1)}, pred[4]{0:T(512)(128)(4,1)S(1)}, u32[]{:S(2)}) copy-start(pred[4]{0:T(512)(128)(4,1)S(1)} %get-tuple-element.435) | copy-start | bytes 16
  29.2 4.3 copy-start.5
  35.9 16.8 %copy-start.2 = (bf16[2,32,32,128]{3,2,1,0:T(8,128)(2,1)S(1)}, bf16[2,32,32,128]{3,2,1,0:T(8,128)(2,1)}, u32[]{:S(2)}) copy-start(bf16[2,32,32,128]{3,2,1,0:T(8,128)(2,1)} %get-tuple-element.325) | copy-start | bytes 1572868
  36.0 17.7 %copy-start.4 = (bf16[2,32,32,128]{3,2,1,0:T(8,128)(2,1)S(1)}, bf16[2,32,32,128]{3,2,1,0:T(8,128)(2,1)}, u32[]{:S(2)}) copy-start(bf16[2,32,32,128]{3,2,1,0:T(8,128)(2,1)} %get-tuple-element.357) | copy-start | bytes 1572868
  36.0 18.5 %copy-start.3 = (bf16[2,32,32,128]{3,2,1,0:T(8,128)(2,1)S(1)}, bf16[2,32,32,128]{3,2,1,0:T(8,128)(2,1)}, u32[]{:S(2)}) copy-start(bf16[2,32,32,128]{3,2,1,0:T(8,128)(2,1)} %get-tuple-element.356) | copy-start | bytes 1572868
  36.0 19.5 %copy-start.1 = (bf16[2,32,32,128]{3,2,1,0:T(8,128)(2,1)S(1)}, bf16[2,32,32,128]{3,2,1,0:T(8,128)(2,1)}, u32[]{:S(2)}) copy-start(bf16[2,32,32,128]{3,2,1,0:T(8,128)(2,1)} %get-tuple-element.354) | copy-start | bytes 1572868
  36.1 27.0 %collective-permute-start.4 = (bf16[2,32,128]{2,1,0:T(8,128)(2,1)S(1)}, bf16[2,32,128]{2,1,0:T(8,128)(2,1)S(1)}, u32[]{:S(2)}, u32[]{:S(2)}) collective-permute-start(bf16[2,32,128]{2,1,0:T(8,128)(2,1)S(1)} %get-tuple-element.392), channel_id=1, source_target_pairs={{0,2},{2,4},{4,6},{6,8},{8,10},{10,12},{12,14},{14,16},{16,18},{18... | collective-permute-start | bytes 49160 | tf_op jit(solution)/shard_map/ppermute | solution.py:15
  36.2 26.9 %collective-permute-start.7 = (bf16[2,32,128]{2,1,0:T(8,128)(2,1)S(1)}, bf16[2,32,128]{2,1,0:T(8,128)(2,1)S(1)}, u32[]{:S(2)}, u32[]{:S(2)}) collective-permute-start(bf16[2,32,128]{2,1,0:T(8,128)(2,1)S(1)} %get-tuple-element.393), channel_id=1, source_target_pairs={{0,16},{2,18},{4,20},{6,22},{8,24},{10,26},{12,28},{14,30},{16,32}... | collective-permute-start | bytes 49160 | tf_op jit(solution)/shard_map/ppermute | solution.py:15
  36.3 26.8 %collective-permute-start.6 = (bf16[2,32,128]{2,1,0:T(8,128)(2,1)S(1)}, bf16[2,32,128]{2,1,0:T(8,128)(2,1)S(1)}, u32[]{:S(2)}, u32[]{:S(2)}) collective-permute-start(bf16[2,32,128]{2,1,0:T(8,128)(2,1)S(1)} %get-tuple-element.394), channel_id=1, source_target_pairs={{0,254},{2,0},{4,2},{6,4},{8,6},{10,8},{12,10},{14,12},{16,14},{18... | collective-permute-start | bytes 49160 | tf_op jit(solution)/shard_map/ppermute | solution.py:15
  40.0 23.0 %collective-permute-start.5 = (bf16[2,32,128]{2,1,0:T(8,128)(2,1)S(1)}, bf16[2,32,128]{2,1,0:T(8,128)(2,1)S(1)}, u32[]{:S(2)}, u32[]{:S(2)}) collective-permute-start(bf16[2,32,128]{2,1,0:T(8,128)(2,1)S(1)} %get-tuple-element.395), channel_id=1, source_target_pairs={{0,240},{2,242},{4,244},{6,246},{8,248},{10,250},{12,252},{14,254}... | collective-permute-start | bytes 49160 | tf_op jit(solution)/shard_map/ppermute | solution.py:15
  66.4 4.9 copy-start.6
  66.4 4.9 copy-start.38
  66.4 4.9 copy-start.39
  96.9 15.9 %collective-permute-start.8 = (bf16[2,32,128]{2,1,0:T(8,128)(2,1)S(1)}, bf16[2,32,128]{2,1,0:T(8,128)(2,1)S(1)}, u32[]{:S(2)}, u32[]{:S(2)}) collective-permute-start(bf16[2,32,128]{2,1,0:T(8,128)(2,1)S(1)} %get-tuple-element.382), channel_id=1, source_target_pairs={{0,2},{2,4},{4,6},{6,8},{8,10},{10,12},{12,14},{14,16},{16,18},{18... | collective-permute-start | bytes 49160 | tf_op jit(solution)/shard_map/ppermute | solution.py:15
  97.0 15.8 %collective-permute-start.11 = (bf16[2,32,128]{2,1,0:T(8,128)(2,1)S(1)}, bf16[2,32,128]{2,1,0:T(8,128)(2,1)S(1)}, u32[]{:S(2)}, u32[]{:S(2)}) collective-permute-start(bf16[2,32,128]{2,1,0:T(8,128)(2,1)S(1)} %get-tuple-element.383), channel_id=1, source_target_pairs={{0,16},{2,18},{4,20},{6,22},{8,24},{10,26},{12,28},{14,30},{16,32}... | collective-permute-start | bytes 49160 | tf_op jit(solution)/shard_map/ppermute | solution.py:15
  97.1 15.8 %collective-permute-start.10 = (bf16[2,32,128]{2,1,0:T(8,128)(2,1)S(1)}, bf16[2,32,128]{2,1,0:T(8,128)(2,1)S(1)}, u32[]{:S(2)}, u32[]{:S(2)}) collective-permute-start(bf16[2,32,128]{2,1,0:T(8,128)(2,1)S(1)} %get-tuple-element.384), channel_id=1, source_target_pairs={{0,254},{2,0},{4,2},{6,4},{8,6},{10,8},{12,10},{14,12},{16,14},{18... | collective-permute-start | bytes 49160 | tf_op jit(solution)/shard_map/ppermute | solution.py:15
  100.8 12.0 collective-permute-start.9
  106.8 6.0 copy-start.15
  106.8 6.1 copy-start.17
  106.8 6.1 copy-start.19
  106.8 6.1 copy-start.21
  106.8 6.2 copy-start.31
  117.4 2.6 copy-start.23
  117.4 2.6 copy-start.25
  117.4 2.6 copy-start.27
  117.4 2.6 copy-start.29
  119.5 5.2 copy-start.33
  119.5 15.2 %copy-start.40 = (f32[128]{0:T(128)S(1)}, f32[128]{0:T(128)}, u32[]{:S(2)}) copy-start(f32[128]{0:T(128)} %get-tuple-element.320) | copy-start | bytes 1540
  124.7 1330.9 %all-reduce.11.cloned.1.call-start = ((), (), s32[]{:S(2)}) async-start(), calls=%async_computation.1 | async-start | bytes 2359296 | tf_op jit(solution)/shard_map/psum | solution.py:213
  124.9 330.8 %collective-permute-start.12 = (bf16[2,32,128]{2,1,0:T(8,128)(2,1)S(1)}, bf16[2,32,128]{2,1,0:T(8,128)(2,1)S(1)}, u32[]{:S(2)}, u32[]{:S(2)}) collective-permute-start(bf16[2,32,128]{2,1,0:T(8,128)(2,1)S(1)} %get-tuple-element.378), channel_id=1, source_target_pairs={{0,2},{2,4},{4,6},{6,8},{8,10},{10,12},{12,14},{14,16},{16,18},{18... | collective-permute-start | bytes 49160 | tf_op jit(solution)/shard_map/ppermute | solution.py:15
  124.9 330.8 %collective-permute-start.15 = (bf16[2,32,128]{2,1,0:T(8,128)(2,1)S(1)}, bf16[2,32,128]{2,1,0:T(8,128)(2,1)S(1)}, u32[]{:S(2)}, u32[]{:S(2)}) collective-permute-start(bf16[2,32,128]{2,1,0:T(8,128)(2,1)S(1)} %get-tuple-element.379), channel_id=1, source_target_pairs={{0,16},{2,18},{4,20},{6,22},{8,24},{10,26},{12,28},{14,30},{16,32}... | collective-permute-start | bytes 49160 | tf_op jit(solution)/shard_map/ppermute | solution.py:15
  125.0 330.7 %collective-permute-start.14 = (bf16[2,32,128]{2,1,0:T(8,128)(2,1)S(1)}, bf16[2,32,128]{2,1,0:T(8,128)(2,1)S(1)}, u32[]{:S(2)}, u32[]{:S(2)}) collective-permute-start(bf16[2,32,128]{2,1,0:T(8,128)(2,1)S(1)} %get-tuple-element.380), channel_id=1, source_target_pairs={{0,254},{2,0},{4,2},{6,4},{8,6},{10,8},{12,10},{14,12},{16,14},{18... | collective-permute-start | bytes 49160 | tf_op jit(solution)/shard_map/ppermute | solution.py:15
  128.8 327.0 %collective-permute-start.13 = (bf16[2,32,128]{2,1,0:T(8,128)(2,1)S(1)}, bf16[2,32,128]{2,1,0:T(8,128)(2,1)S(1)}, u32[]{:S(2)}, u32[]{:S(2)}) collective-permute-start(bf16[2,32,128]{2,1,0:T(8,128)(2,1)S(1)} %get-tuple-element.381), channel_id=1, source_target_pairs={{0,240},{2,242},{4,244},{6,246},{8,248},{10,250},{12,252},{14,254}... | collective-permute-start | bytes 49160 | tf_op jit(solution)/shard_map/ppermute | solution.py:15
  (11 other events, 17.5 us)
Sparse Core Ops, SparseCore 0:
  124.8 1256.8 all-reduce.8
  1384.3 71.1 all-reduce.10
